TPU v7x, 32 devices: a whole 2x2x4 slice. The times are simulated.
32 devices in a mesh: shard: 2 (over y), blk: 4 (over z), ckpt: 2 (over x), qry: 2 (over core).
Axes of the slice: x: 2, y: 2, z: 4, core: 2. Of those that a mesh axis runs over, the one named last changes fastest.
Arguments:
- query_feats: bfloat16 [2, 8192, 2048], P('ckpt', ('shard', 'blk', 'qry')), parts along dimension 1, may hold values from -6 to 6
- train_feats: bfloat16 [2, 1024, 2048], P('ckpt', ('shard', 'blk')), parts along dimension 1, may hold values from -0.125 to 0.125
- loss_weights: bfloat16 [2, 1024], P('ckpt', ('shard', 'blk')), parts along dimension 1, may hold values from 0.099609375 to 1
- pair_list: int32 [32, 2], P(('shard', 'blk', 'qry')), parts along dimension 0, may hold values from 0 to 3, all different within a row
- tile_owner: int32 [8], P('shard'), parts along dimension 0, may hold values from 0 to 3, each once
Outputs:
- scores: float32 [8192, 512], P(('shard', 'blk', 'qry'), 'ckpt'), parts along dimension 0
There are 2 independent parts, one for each index of `shard`. A program takes and returns all parts, laid end to end along the dimension named above; each array names one. Nothing has to cross between parts.
Inputs may be any that keep to these rules, and one draw needn't show every extreme that they name: `pair_list`: each row names 2 different training blocks; every training block is named by some row. `tile_owner`: a permutation of the training blocks.
All inputs are finite; a program needn't handle non-finite values.
Results may differ from a plain program's by a relative error of at most 0.0003.
Values may be sent and summed in bfloat16 or wider, within the bound.
No kernel may reach another device: no remote copies, remote signals or barrier semaphores. Data moves between devices by JAX's collectives and lax.ppermute only.
A program may use at most 128 MiB of HBM per device.

v0:
```python
import jax
import jax.numpy as jnp
from jax import lax
from jax.sharding import PartitionSpec as P

QBLK = 256
TBLK = 128


def per_device(query_feats, train_feats, loss_weights, pair_list, tile_owner):
    queries = query_feats[0]
    block_count = lax.axis_size("blk")
    total_rows = TBLK * block_count
    block_ids = jnp.arange(block_count, dtype=jnp.int32)
    wanted = jnp.any(pair_list[:, :, None] == block_ids[None, None, :], axis=1).astype(jnp.float32)
    own_rows = train_feats[0]
    own_weights = loss_weights[0]
    gathered_rows, gathered_weights = (
        lax.all_gather(own_rows, "blk", axis=0, tiled=True),
        lax.all_gather(own_weights, "blk", axis=0, tiled=True),
    )
    row_blocks = gathered_rows.reshape(block_count, TBLK, gathered_rows.shape[1])
    weight_blocks = gathered_weights.reshape(block_count, TBLK)
    query_mask = jnp.transpose(jnp.repeat(wanted, QBLK, axis=0))
    owner_rows = total_rows // lax.axis_size("ckpt")
    picked = row_blocks[tile_owner].reshape(lax.axis_size("ckpt") * owner_rows, row_blocks.shape[2])
    picked_weights = (
        weight_blocks[tile_owner].reshape(lax.axis_size("ckpt") * owner_rows).astype(jnp.float32)
    )
    products = lax.dot_general(
        picked, queries, (((1,), (1,)), ((), ())), preferred_element_type=jnp.float32
    )
    mask_rows = jnp.repeat(query_mask[tile_owner], TBLK, axis=0)
    summed_rows = lax.psum_scatter(
        products * picked_weights[:, None] * mask_rows, "ckpt", scatter_dimension=0, tiled=True
    )
    return jnp.transpose(summed_rows)


def solution(mesh):
    return jax.shard_map(
        per_device,
        mesh=mesh,
        in_specs=(
            P("ckpt", ("shard", "blk", "qry"), None),
            P("ckpt", ("shard", "blk"), None),
            P("ckpt", ("shard", "blk")),
            P(("shard", "blk", "qry"), None),
            P("shard"),
        ),
        out_specs=P(("shard", "blk", "qry"), "ckpt"),
        check_vma=False,
    )
```

profile of v0, /device:TPU:0, one launch (start us, length us, event | category | flops | bytes accessed | tf_op | source)
XLA Modules:
  0.0 93.2 jit_solution(14550216381288683997)
XLA Ops:
  6.5 0.0 copy-start
  6.5 0.0 all-gather.4.cloned.1.call-start
  6.5 0.7 all-gather.4.cloned.1.call-update
  7.3 0.0 reduce-scatter.2.cloned.1.call-start
  7.3 0.8 compare_reduce_fusion
  8.1 0.1 copy.7
  8.2 0.1 broadcast_bitcast_fusion
  8.3 0.7 compare_select_fusion
  8.9 0.6 gather_fusion.2
  9.5 12.8 %all-gather.1 = bf16[1,512]{1,0:T(2,128)(2,1)S(1)} all-gather(bf16[1,128]{1,0:T(2,128)(2,1)} %param.7), channel_id=3, replica_groups=mesh['shard'=2,'blk'=4,'ckpt'=2,'qry'=2] {'blk'}, dimensions={1}, use_global_device_ids=true | all-gather | bytes 1280 | tf_op jit(solution)/shard_map/all_gather | solution.py:20
  22.3 0.6 gather_fusion.1
  22.9 34.4 %all-gather.4.cloned.1.call-done = bf16[1,512,2048]{2,1,0:T(8,128)(2,1)} async-done(((bf16[1,128,2048]{2,1,0:T(8,128)(2,1)}), bf16[1,512,2048]{2,1,0:T(8,128)(2,1)}) %all-gather.4.cloned.1.call-update) | async-done | bytes 2097168 | tf_op jit(solution)/shard_map/all_gather | solution.py:19
  57.3 3.6 %gather_fusion = bf16[4,128,2048]{2,1,0:T(8,128)(2,1)} fusion(bf16[4,128,2048]{2,1,0:T(8,128)(2,1)} %bitcast.23, s32[1024]{0:T(1024)S(1)} %pad_clamp_fusion), kind=kCustom, calls=%fused_computation | custom fusion | bytes 4194320 | tf_op jit(solution)/shard_map/gather | solution.py:26
  60.9 0.1 broadcast_in_dim.16
  61.1 0.0 copy-done
  61.1 3.9 %fusion.5 = f32[512,512]{1,0:T(8,128)} fusion(f32[512,512]{1,0:T(8,128)S(1)} %bitcast.25, bf16[512,2048]{1,0:T(8,128)(2,1)} %bitcast.24, bf16[1,512,2048]{2,1,0:T(8,128)(2,1)S(1)} %copy-done, f32[512]{0:T(512)S(1)} %bitcast_convert_fusion), kind=kOutput, calls=%fused_computation.6 | convolution fusion | flops 1074266112 | bytes 6293504 | tf_op jit(solution)/shard_map/dot_general | solution.py:30
  64.9 0.0 reduce-scatter.2.cloned.1.call-update
  65.0 19.3 %reduce-scatter.2.cloned.1.call-done = f32[256,512]{1,0:T(8,128)} async-done(((f32[512,512]{1,0:T(8,128)}), f32[256,512]{1,0:T(8,128)}) %reduce-scatter.2.cloned.1.call-update) | async-done | bytes 524304 | tf_op jit(solution)/shard_map/reduce_scatter | solution.py:34
  84.3 2.0 %copy.8 = f32[512,256]{1,0:T(8,128)} copy(f32[512,256]{0,1:T(8,128)} %bitcast.27) | data formatting | bytes 1048576 | tf_op jit(solution)/shard_map/transpose | solution.py:37
  (5 shorter events, 0.0 us)
Async XLA Ops:
  6.5 54.5 %copy-start = (bf16[1,512,2048]{2,1,0:T(8,128)(2,1)S(1)}, bf16[1,512,2048]{2,1,0:T(8,128)(2,1)}, u32[]{:S(2)}) copy-start(bf16[1,512,2048]{2,1,0:T(8,128)(2,1)} %param.5) | copy-start | bytes 6291460
  6.5 50.8 %all-gather.4.cloned.1.call-start = ((), (), s32[]{:S(2)}) async-start(), calls=%async_computation.2 | async-start | bytes 2621440 | tf_op jit(solution)/shard_map/all_gather | solution.py:19
  7.3 77.0 %reduce-scatter.2.cloned.1.call-start = ((), (), s32[]{:S(2)}) async-start(), calls=%async_computation.1 | async-start | bytes 1572864 | tf_op jit(solution)/shard_map/reduce_scatter | solution.py:34
Sparse Core Ops, SparseCore 0:
  8.9 48.3 all-gather.3
  65.1 19.1 reduce-scatter.1
where the time goes:
time: 93.4 us; the launch traced here: 93.2 us
  waiting for transfers between devices  54.5 us (58%)
  between operations  13.4 us (14%)
  blocking collectives  12.8 us (14%)
  local copies, waits for them, and re-layouts  7.07 us (8%)
  matrix products  3.86 us (4%)
  other arithmetic  1.47 us (2%)
    all_gather x1, waiting for transfers between devices, per_device(): lax.all_gather(own_rows, 'blk', axis=0, tiled=True)  34.4 us
    reduce_scatter x1, waiting for transfers between devices, per_device(): lax.psum_scatter(products * picked_weights[:, None] * mask_rows, 'ckpt',...  19.3 us
    all_gather x1, blocking collectives, per_device(): lax.all_gather(own_weights, 'blk', axis=0, tiled=True)  12.8 us
    dot_general x1, matrix products, per_device(): lax.dot_general(picked, queries, (((1,), (1,)), ((), ())), preferred_elem...  3.86 us
    gather x1, local copies, waits for them, and re-layouts, per_device(): row_blocks[tile_owner]  3.62 us
    transpose x1, local copies, waits for them, and re-layouts, per_device(): return jnp.transpose(summed_rows)  2.04 us
  transfers between devices with their start and end apart: 2, of which 2 were waited for; matrix products, arithmetic and copies ran while one was open for 3% of the time, Pallas kernels for 0%

commit v1 on v0

--- a/solution.py
+++ b/solution.py
@@ -5,6 +5,28 @@
 
 QBLK = 256
 TBLK = 128
+
+
+def tracks_plan(w_in, array_axis):
+    formed = list(w_in.shape[1:])
+    formed[array_axis] *= w_in.shape[0]
+    return jnp.moveaxis(w_in, 0, array_axis).reshape(formed)
+
+
+def advance_steps_all_in(frame, peer_axis):
+    known = lax.axis_size(peer_axis)
+    block_last = lax.axis_index(peer_axis)
+    built, w1 = (known, block_last)
+    moved, item_now = (frame[None], 1)
+    while item_now < built:
+        near = tuple(((u, u ^ item_now) for u in range(built)))
+        out_arr = lax.ppermute(moved, peer_axis, perm=near)
+        tall = w1 & item_now == 0
+        z_new = jnp.where(tall, moved, out_arr)
+        parts_out = jnp.where(tall, out_arr, moved)
+        moved = jnp.concatenate([z_new, parts_out])
+        item_now *= 2
+    return moved
 
 
 def per_device(query_feats, train_feats, loss_weights, pair_list, tile_owner):
@@ -15,8 +37,13 @@
     wanted = jnp.any(pair_list[:, :, None] == block_ids[None, None, :], axis=1).astype(jnp.float32)
     own_rows = train_feats[0]
     own_weights = loss_weights[0]
+
+    def store_screen(u_in, in_array, out_dim):
+        frame_out = advance_steps_all_in(in_array, u_in)
+        return tracks_plan(frame_out, out_dim)
+
     gathered_rows, gathered_weights = (
-        lax.all_gather(own_rows, "blk", axis=0, tiled=True),
+        store_screen("blk", in_array=own_rows, out_dim=0),
         lax.all_gather(own_weights, "blk", axis=0, tiled=True),
     )
     row_blocks = gathered_rows.reshape(block_count, TBLK, gathered_rows.shape[1])

time: 93.4 us -> 116 us (1.24)
  blocking collectives: 12.8 us -> 26.8 us
  starting transfers between devices: 0.04 us -> 5.81 us
  other arithmetic: 1.47 us -> 5.32 us
    all_gather x1 -> x0, waiting for transfers between devices: 34.4 us -> none  [per_device(): lax.all_gather(own_rows, 'blk', axis=0, tiled=True)]
    ppermute x0 -> x2, waiting for transfers between devices: none -> 29.2 us  [advance_steps_all_in(): out_arr = lax.ppermute(moved, peer_axis, perm=near)]
    all_gather x1, blocking collectives: 12.8 us -> 26.8 us  [per_device(): lax.all_gather(own_weights, 'blk', axis=0, tiled=True)]
    ppermute x0 -> x2, starting transfers between devices: none -> 5.81 us  [advance_steps_all_in(): out_arr = lax.ppermute(moved, peer_axis, perm=near)]
    reduce_scatter x1, waiting for transfers between devices: 19.3 us -> 24.2 us  [per_device(): lax.psum_scatter(products * picked_weights[:, None] * mask_rows, 'ckpt',...]
    select_n x0 -> x2, other arithmetic: none -> 2.64 us  [advance_steps_all_in(): z_new = jnp.where(tall, moved, out_arr)]
    concatenate x0 -> x2, other arithmetic: none -> 2.55 us  [advance_steps_all_in(): moved = jnp.concatenate([z_new, parts_out])]
  transfers between devices with their start and end apart: 2 -> 3, of which waited for: 2 -> 3; matrix products, arithmetic and copies ran while one was open for 3% -> 1% of each run, Pallas kernels for 0% -> 0%
where the time goes in v1:
time: 116 us
  waiting for transfers between devices  53.4 us (46%)
  blocking collectives  26.8 us (23%)
  between operations  13.4 us (12%)
  local copies, waits for them, and re-layouts  7.07 us (6%)
  starting transfers between devices  5.81 us (5%)
  other arithmetic  5.32 us (5%)
  matrix products  3.88 us (3%)
    ppermute x2, waiting for transfers between devices, advance_steps_all_in(): out_arr = lax.ppermute(moved, peer_axis, perm=near)  29.2 us
    all_gather x1, blocking collectives, per_device(): lax.all_gather(own_weights, 'blk', axis=0, tiled=True)  26.8 us
    reduce_scatter x1, waiting for transfers between devices, per_device(): lax.psum_scatter(products * picked_weights[:, None] * mask_rows, 'ckpt',...  24.2 us
    ppermute x2, starting transfers between devices, advance_steps_all_in(): out_arr = lax.ppermute(moved, peer_axis, perm=near)  5.81 us
    dot_general x1, matrix products, per_device(): lax.dot_general(picked, queries, (((1,), (1,)), ((), ())), preferred_elem...  3.88 us
    gather x1, local copies, waits for them, and re-layouts, per_device(): row_blocks[tile_owner]  3.61 us
    select_n x2, other arithmetic, advance_steps_all_in(): z_new = jnp.where(tall, moved, out_arr)  2.64 us
    concatenate x2, other arithmetic, advance_steps_all_in(): moved = jnp.concatenate([z_new, parts_out])  2.55 us
  transfers between devices with their start and end apart: 3, of which 3 were waited for; matrix products, arithmetic and copies ran while one was open for 1% of the time, Pallas kernels for 0%

profile of v1, /device:TPU:0, one launch (start us, length us, event | category | flops | bytes accessed | tf_op | source)
XLA Modules:
  0.0 115.8 jit_solution(1013740103934778733)
XLA Ops:
  6.5 0.0 copy-start
  6.5 0.0 reduce-scatter.2.cloned.1.call-start
  6.5 3.1 %collective-permute-start = (bf16[1,128,2048]{2,1,0:T(8,128)(2,1)}, bf16[1,128,2048]{2,1,0:T(8,128)(2,1)}, u32[]{:S(2)}, u32[]{:S(2)}) collective-permute-start(bf16[1,128,2048]{2,1,0:T(8,128)(2,1)} %param.6), channel_id=1, source_target_pairs={{0,4},{4,0},{8,12},{12,8},{1,5},{5,1},{9,13},{13,9},{2,6},{6,2},{1... | collective-permute-start | bytes 1572872 | tf_op jit(solution)/shard_map/ppermute | solution.py:23
  9.6 0.0 copy-start.2
  9.6 0.0 copy-start.3
  9.6 0.0 copy-start.1
  9.6 12.2 %collective-permute-done = bf16[1,128,2048]{2,1,0:T(8,128)(2,1)} collective-permute-done((bf16[1,128,2048]{2,1,0:T(8,128)(2,1)}, bf16[1,128,2048]{2,1,0:T(8,128)(2,1)}, u32[]{:S(2)}, u32[]{:S(2)}) %collective-permute-start) | collective-permute-done | bytes 524320 | tf_op jit(solution)/shard_map/ppermute | solution.py:23
  21.8 1.3 %broadcast_select_fusion.3 = (bf16[1,128,2048]{2,1,0:T(8,128)(2,1)S(1)}, bf16[1,128,2048]{2,1,0:T(8,128)(2,1)S(1)}) fusion(bf16[1,128,2048]{2,1,0:T(8,128)(2,1)} %param.6, bf16[1,128,2048]{2,1,0:T(8,128)(2,1)} %collective-permute-done, pred[]{:T(512)S(6)} %eq.20), kind=kLoop, calls=%fused_computation.12 | loop fusion | flops 524288 | bytes 2097153 | tf_op jit(solution)/shard_map/jit(_where)/select_n | solution.py:25
  23.1 1.1 pad_maximum_fusion.1
  24.2 2.8 %collective-permute-start.1 = (bf16[2,128,2048]{2,1,0:T(8,128)(2,1)}, bf16[2,128,2048]{2,1,0:T(8,128)(2,1)}, u32[]{:S(2)}, u32[]{:S(2)}) collective-permute-start(bf16[2,128,2048]{2,1,0:T(8,128)(2,1)} %pad_maximum_fusion.1), channel_id=1, source_target_pairs={{0,8},{4,12},{8,0},{12,4},{1,9},{5,13},{9,1},{13,5},{2,10},{6,14},... | collective-permute-start | bytes 3145736 | tf_op jit(solution)/shard_map/ppermute | solution.py:23
  26.9 0.0 copy-done.2
  26.9 0.1 compare_reduce_fusion
  27.0 0.1 copy.7
  27.1 0.1 broadcast_bitcast_fusion
  27.2 0.0 copy-done.3
  27.2 0.6 gather_fusion.2
  27.8 0.0 copy-done.1
  27.8 26.8 %all-gather = bf16[1,512]{1,0:T(2,128)(2,1)S(1)} all-gather(bf16[1,128]{1,0:T(2,128)(2,1)S(1)} %copy-done.1), channel_id=2, replica_groups=mesh['shard'=2,'blk'=4,'ckpt'=2,'qry'=2] {'blk'}, dimensions={1}, use_global_device_ids=true | all-gather | bytes 1280 | tf_op jit(solution)/shard_map/all_gather | solution.py:47
  54.7 0.6 gather_fusion.1
  55.2 17.0 %collective-permute-done.1 = bf16[2,128,2048]{2,1,0:T(8,128)(2,1)} collective-permute-done((bf16[2,128,2048]{2,1,0:T(8,128)(2,1)}, bf16[2,128,2048]{2,1,0:T(8,128)(2,1)}, u32[]{:S(2)}, u32[]{:S(2)}) %collective-permute-start.1) | collective-permute-done | bytes 1048608 | tf_op jit(solution)/shard_map/ppermute | solution.py:23
  72.2 1.4 %broadcast_select_fusion.1 = (bf16[2,128,2048]{2,1,0:T(8,128)(2,1)S(1)}, bf16[2,128,2048]{2,1,0:T(8,128)(2,1)S(1)}) fusion(bf16[2,128,2048]{2,1,0:T(8,128)(2,1)} %collective-permute-done.1, pred[]{:T(512)S(6)} %eq.19, bf16[1,128,2048]{2,1,0:T(8,128)(2,1)S(1)} %get-tuple-element.8, bf16[1,128,2048]{2,1,0:T(8,128)(2,1)S(1)} %get-tuple-element.7), kind=kLoop, calls=%fused_computation.10 | loop fusion | flops 1572864 | bytes 4194305 | tf_op jit(solution)/shard_map/jit(_where)/select_n | solution.py:25
  73.6 1.5 %pad_maximum_fusion = bf16[4,128,2048]{2,1,0:T(8,128)(2,1)} fusion(bf16[2,128,2048]{2,1,0:T(8,128)(2,1)S(1)} %get-tuple-element.6, bf16[2,128,2048]{2,1,0:T(8,128)(2,1)S(1)} %get-tuple-element.5), kind=kLoop, calls=%fused_computation.3 | loop fusion | flops 1048576 | bytes 4194304 | tf_op jit(solution)/shard_map/concatenate | solution.py:27
  75.1 3.6 %gather_fusion = bf16[4,128,2048]{2,1,0:T(8,128)(2,1)} fusion(bf16[4,128,2048]{2,1,0:T(8,128)(2,1)} %pad_maximum_fusion, s32[1024]{0:T(1024)S(1)} %pad_clamp_fusion), kind=kCustom, calls=%fused_computation | custom fusion | bytes 4194320 | tf_op jit(solution)/shard_map/gather | solution.py:53
  78.7 0.1 broadcast_in_dim.16
  78.8 0.0 copy-done
  78.8 3.9 %fusion.5 = f32[512,512]{1,0:T(8,128)} fusion(f32[512,512]{1,0:T(8,128)S(1)} %bitcast.23, bf16[512,2048]{1,0:T(8,128)(2,1)} %bitcast.22, bf16[1,512,2048]{2,1,0:T(8,128)(2,1)S(1)} %copy-done, f32[512]{0:T(512)S(1)} %bitcast_convert_fusion), kind=kOutput, calls=%fused_computation.7 | convolution fusion | flops 1074266112 | bytes 6293504 | tf_op jit(solution)/shard_map/dot_general | solution.py:57
  82.7 0.0 reduce-scatter.2.cloned.1.call-update
  82.7 24.2 %reduce-scatter.2.cloned.1.call-done = f32[256,512]{1,0:T(8,128)} async-done(((f32[512,512]{1,0:T(8,128)}), f32[256,512]{1,0:T(8,128)}) %reduce-scatter.2.cloned.1.call-update) | async-done | bytes 524304 | tf_op jit(solution)/shard_map/reduce_scatter | solution.py:61
  106.9 2.0 %copy.8 = f32[512,256]{1,0:T(8,128)} copy(f32[512,256]{0,1:T(8,128)} %bitcast.25) | data formatting | bytes 1048576 | tf_op jit(solution)/shard_map/transpose | solution.py:64
  (6 shorter events, 0.1 us)
Async XLA Ops:
  6.5 72.3 %copy-start = (bf16[1,512,2048]{2,1,0:T(8,128)(2,1)S(1)}, bf16[1,512,2048]{2,1,0:T(8,128)(2,1)}, u32[]{:S(2)}) copy-start(bf16[1,512,2048]{2,1,0:T(8,128)(2,1)} %param.5) | copy-start | bytes 6291460
  6.5 100.3 %reduce-scatter.2.cloned.1.call-start = ((), (), s32[]{:S(2)}) async-start(), calls=%async_computation.1 | async-start | bytes 1572864 | tf_op jit(solution)/shard_map/reduce_scatter | solution.py:61
  6.5 15.3 %collective-permute-start = (bf16[1,128,2048]{2,1,0:T(8,128)(2,1)}, bf16[1,128,2048]{2,1,0:T(8,128)(2,1)}, u32[]{:S(2)}, u32[]{:S(2)}) collective-permute-start(bf16[1,128,2048]{2,1,0:T(8,128)(2,1)} %param.6), channel_id=1, source_target_pairs={{0,4},{4,0},{8,12},{12,8},{1,5},{5,1},{9,13},{13,9},{2,6},{6,2},{1... | collective-permute-start | bytes 1572872 | tf_op jit(solution)/shard_map/ppermute | solution.py:23
  9.6 17.3 %copy-start.2 = (s32[2,2]{1,0:T(2,128)S(1)}, s32[2,2]{1,0:T(2,128)}, u32[]{:S(2)}) copy-start(s32[2,2]{1,0:T(2,128)} %param.8) | copy-start | bytes 52
  9.6 17.6 %copy-start.3 = (s32[4]{0:T(128)S(1)}, s32[4]{0:T(128)}, u32[]{:S(2)}) copy-start(s32[4]{0:T(128)} %param.9) | copy-start | bytes 52
  9.6 18.2 %copy-start.1 = (bf16[1,128]{1,0:T(2,128)(2,1)S(1)}, bf16[1,128]{1,0:T(2,128)(2,1)}, u32[]{:S(2)}) copy-start(bf16[1,128]{1,0:T(2,128)(2,1)} %param.7) | copy-start | bytes 772
  24.2 48.0 %collective-permute-start.1 = (bf16[2,128,2048]{2,1,0:T(8,128)(2,1)}, bf16[2,128,2048]{2,1,0:T(8,128)(2,1)}, u32[]{:S(2)}, u32[]{:S(2)}) collective-permute-start(bf16[2,128,2048]{2,1,0:T(8,128)(2,1)} %pad_maximum_fusion.1), channel_id=1, source_target_pairs={{0,8},{4,12},{8,0},{12,4},{1,9},{5,13},{9,1},{13,5},{2,10},{6,14},... | collective-permute-start | bytes 3145736 | tf_op jit(solution)/shard_map/ppermute | solution.py:23
Sparse Core Ops, SparseCore 0:
  82.8 24.0 reduce-scatter.1
